TPU v7x, 32 devices: a whole 2x2x4 slice. The times are simulated.
32 devices in a mesh: dp: 8 (over z, x), space: 4 (over y, core).
Axes of the slice: x: 2, y: 2, z: 4, core: 2. Of those that a mesh axis runs over, the one named last changes fastest.
Arguments:
- images: bfloat16 [256, 24, 24, 384], P('dp', 'space'), may hold values from -6 to 6
- cotangent: bfloat16 [256, 24, 24, 384], P('dp', 'space'), may hold values from -6 to 6
- image_sides: int32 [256], P('dp'), may hold values from 14 to 24, as said below
- keep_flags: int32 [256], P('dp'), may hold values 0 or 1
- depth_kernel: float32 [49, 384], P(None, ('dp', 'space')), may hold values from -0.875 to 0.875
- kernel_moment: float32 [49, 384], P(None, ('dp', 'space')), may hold values from -0.00061035156 to 0.00061035156
- kernel_square: float32 [49, 384], P(None, ('dp', 'space')), may hold values from 4.1600107e-10 to 6.656017e-09
- block_vectors: float32 [5, 384], P(None, ('dp', 'space')), may hold values from -1.5 to 1.5
- vector_moment: float32 [5, 384], P(None, ('dp', 'space')), may hold values from -0.00061035156 to 0.00061035156
- vector_square: float32 [5, 384], P(None, ('dp', 'space')), may hold values from 4.1600107e-10 to 6.656017e-09
- up_weight: float32 [384, 1536], P(None, ('dp', 'space')), may hold values from -0.3125 to 0.3125
- up_moment: float32 [384, 1536], P(None, ('dp', 'space')), may hold values from -0.00061035156 to 0.00061035156
- up_square: float32 [384, 1536], P(None, ('dp', 'space')), may hold values from 4.1600107e-10 to 6.656017e-09
- up_bias: float32 [1536], P(('dp', 'space')), may hold values from -3 to 3
- bias_moment: float32 [1536], P(('dp', 'space')), may hold values from -0.00061035156 to 0.00061035156
- bias_square: float32 [1536], P(('dp', 'space')), may hold values from 4.1600107e-10 to 6.656017e-09
- down_weight: float32 [1536, 384], P(('dp', 'space')), may hold values from -0.15625 to 0.15625
- down_moment: float32 [1536, 384], P(('dp', 'space')), may hold values from -0.00061035156 to 0.00061035156
- down_square: float32 [1536, 384], P(('dp', 'space')), may hold values from 4.1600107e-10 to 6.656017e-09
Outputs:
- out_images: bfloat16 [256, 24, 24, 384], P('dp', 'space')
- grad_images: bfloat16 [256, 24, 24, 384], P('dp', 'space')
- new_kernel: float32 [49, 384], P(None, ('dp', 'space'))
- new_kernel_moment: float32 [49, 384], P(None, ('dp', 'space'))
- new_kernel_square: float32 [49, 384], P(None, ('dp', 'space'))
- new_vectors: float32 [5, 384], P(None, ('dp', 'space'))
- new_vector_moment: float32 [5, 384], P(None, ('dp', 'space'))
- new_vector_square: float32 [5, 384], P(None, ('dp', 'space'))
- new_up: float32 [384, 1536], P(None, ('dp', 'space'))
- new_up_moment: float32 [384, 1536], P(None, ('dp', 'space'))
- new_up_square: float32 [384, 1536], P(None, ('dp', 'space'))
- new_bias: float32 [1536], P(('dp', 'space'))
- new_bias_moment: float32 [1536], P(('dp', 'space'))
- new_bias_square: float32 [1536], P(('dp', 'space'))
- new_down: float32 [1536, 384], P(('dp', 'space'))
- new_down_moment: float32 [1536, 384], P(('dp', 'space'))
- new_down_square: float32 [1536, 384], P(('dp', 'space'))
- grad_norm: float32 [], replicated
Inputs may be any that keep to these rules, and one draw needn't show every extreme that they name: `image_sides`: each image's valid square has one of the sides 24, 18, 14.
All inputs are finite; a program needn't handle non-finite values. No bound on the sum of `keep_flags` on one device may be relied on, other than what follows from the above.
Results may differ from a plain program's by a relative error of at most 0.0055.
Values may be sent and summed in bfloat16 or wider, within the bound.
No kernel may reach another device: no remote copies, remote signals or barrier semaphores. Data moves between devices by JAX's collectives and lax.ppermute only.
A program may use at most 192 MiB of HBM per device.

v0:
```python
import jax
import jax.numpy as jnp
from jax import lax
from jax.sharding import PartitionSpec as P

STEP = 5
keep_scale = 4.0 / 3.0
norm_eps = 1e-06
clip_limit = 1.0
beta_one = 0.9
beta_two = 0.999
adam_eps = 1e-08
decay_rate = 0.05
step_rates = (0.15, 0.5, 0.05, 0.2, 0.025)
inv_root_two = 0.7071067811865476
inv_root_tau = 0.3989422804014327


def conv_rows(padded, kernel, out_rows, out_cols):
    wide = jnp.pad(padded, ((0, 0), (0, 0), (3, 3), (0, 0)))
    running = jnp.zeros((padded.shape[0], out_rows, out_cols, padded.shape[3]), jnp.float32)
    for row_off in range(7):
        for col_off in range(7):
            running = (
                running
                + kernel[row_off * 7 + col_off]
                * wide[:, row_off : row_off + out_rows, col_off : col_off + out_cols, :]
            )
    return running


def kernel_grad(padded, grad_conv):
    wide = jnp.pad(padded, ((0, 0), (0, 0), (3, 3), (0, 0)))
    out_rows = grad_conv.shape[1]
    out_cols = grad_conv.shape[2]
    pieces = [
        jnp.sum(
            wide[:, row_off : row_off + out_rows, col_off : col_off + out_cols, :] * grad_conv,
            axis=(0, 1, 2),
        )
        for row_off in range(7)
        for col_off in range(7)
    ]
    return jnp.stack(pieces)


def adam_update(weight, moment, square, grad_part, factor, step_rate):
    scaled = grad_part * factor
    new_moment = beta_one * moment + (1.0 - beta_one) * scaled
    new_square = beta_two * square + (1.0 - beta_two) * scaled * scaled
    corrected = new_moment / (1.0 - beta_one**STEP)
    spread = jnp.sqrt(new_square / (1.0 - beta_two**STEP))
    new_weight = weight - step_rate * (corrected / (spread + adam_eps) + decay_rate * weight)
    return (new_weight, new_moment, new_square)


def body(
    images,
    cotangent,
    image_sides,
    keep_flags,
    depth_kernel,
    kernel_moment,
    kernel_square,
    block_vectors,
    vector_moment,
    vector_square,
    up_weight,
    up_moment,
    up_square,
    up_bias,
    bias_moment,
    bias_square,
    down_weight,
    down_moment,
    down_square,
):
    up_full, down_full = (
        lax.all_gather(up_weight.astype(jnp.bfloat16), ("dp", "space"), axis=1, tiled=True),
        lax.all_gather(down_weight.astype(jnp.bfloat16), ("dp", "space"), axis=0, tiled=True),
    )
    kernel_full, vector_full, bias_full = (
        lax.all_gather(depth_kernel, ("dp", "space"), axis=1, tiled=True),
        lax.all_gather(block_vectors, ("dp", "space"), axis=1, tiled=True),
        lax.all_gather(up_bias, ("dp", "space"), axis=0, tiled=True),
    )
    map_side = images.shape[2]
    local_images, local_cot = (
        lax.all_to_all(images, "space", split_axis=0, concat_axis=1, tiled=True),
        lax.all_to_all(cotangent, "space", split_axis=0, concat_axis=1, tiled=True),
    )
    img_count = local_images.shape[0]
    first_image = lax.axis_index("space") * img_count
    local_sides = lax.dynamic_slice_in_dim(image_sides, first_image, img_count)
    local_keep = lax.dynamic_slice_in_dim(keep_flags, first_image, img_count)
    row_ids = jnp.arange(map_side, dtype=jnp.int32)
    col_ids = jnp.arange(map_side, dtype=jnp.int32)
    rows_in = row_ids[None, :] < local_sides[:, None]
    cols_in = col_ids[None, :] < local_sides[:, None]
    pixel_mask = (rows_in[:, :, None] & cols_in[:, None, :]).astype(jnp.float32)
    branch_scale = pixel_mask * (local_keep.astype(jnp.float32) * keep_scale)[:, None, None]
    masked = local_images * pixel_mask.astype(jnp.bfloat16)[..., None]
    padded = jnp.pad(masked, ((0, 0), (3, 3), (0, 0), (0, 0)))
    out_rows = local_images.shape[1]
    conv = conv_rows(padded, kernel_full, out_rows, map_side) + vector_full[0]
    chan_mean = jnp.mean(conv, axis=-1, keepdims=True)
    centred = conv - chan_mean
    chan_var = jnp.mean(centred * centred, axis=-1, keepdims=True)
    inv_std = lax.rsqrt(chan_var + norm_eps)
    unit_norm = centred * inv_std
    normed = (unit_norm * vector_full[1] + vector_full[2]).astype(jnp.bfloat16)
    hidden = (
        jnp.einsum("nijc,ch->nijh", normed, up_full, preferred_element_type=jnp.float32) + bias_full
    )
    normal_cdf = 0.5 * (1.0 + lax.erf(hidden * inv_root_two))
    active = (hidden * normal_cdf).astype(jnp.bfloat16)
    branch = (
        jnp.einsum("nijh,hc->nijc", active, down_full, preferred_element_type=jnp.float32)
        + vector_full[3]
    )
    out_images = (
        local_images.astype(jnp.float32) + branch_scale[..., None] * vector_full[4] * branch
    ).astype(jnp.bfloat16)
    grad_out = local_cot.astype(jnp.float32)
    grad_branch = (grad_out * branch_scale[..., None] * vector_full[4]).astype(jnp.bfloat16)
    grad_scale = jnp.sum(grad_out * branch_scale[..., None] * branch, axis=(0, 1, 2))
    grad_outbias = jnp.sum(grad_branch.astype(jnp.float32), axis=(0, 1, 2))
    grad_down = jnp.einsum("nijh,nijc->hc", active, grad_branch, preferred_element_type=jnp.float32)
    grad_active = jnp.einsum(
        "nijc,hc->nijh", grad_branch, down_full, preferred_element_type=jnp.float32
    )
    slope = normal_cdf + hidden * inv_root_tau * jnp.exp(-0.5 * hidden * hidden)
    grad_hidden = (grad_active * slope).astype(jnp.bfloat16)
    grad_up = jnp.einsum("nijc,nijh->ch", normed, grad_hidden, preferred_element_type=jnp.float32)
    grad_upbias = jnp.sum(grad_hidden.astype(jnp.float32), axis=(0, 1, 2))
    grad_normed = jnp.einsum(
        "nijh,ch->nijc", grad_hidden, up_full, preferred_element_type=jnp.float32
    )
    grad_gain = jnp.sum(grad_normed * unit_norm, axis=(0, 1, 2))
    grad_shift = jnp.sum(grad_normed, axis=(0, 1, 2))
    scaled_dn = grad_normed * vector_full[1]
    grad_conv = inv_std * (
        scaled_dn
        - jnp.mean(scaled_dn, axis=-1, keepdims=True)
        - unit_norm * jnp.mean(scaled_dn * unit_norm, axis=-1, keepdims=True)
    )
    grad_convbias = jnp.sum(grad_conv, axis=(0, 1, 2))
    grad_rows = jnp.pad(grad_conv, ((0, 0), (3, 3), (0, 0), (0, 0)))
    grad_u = conv_rows(grad_rows, kernel_full[::-1], out_rows, map_side)
    grad_local = (grad_out + pixel_mask[..., None] * grad_u).astype(jnp.bfloat16)
    grad_kernel = kernel_grad(padded, grad_conv)
    grad_vectors = jnp.stack([grad_convbias, grad_gain, grad_shift, grad_outbias, grad_scale])
    out_tiles, grad_tiles = (
        lax.all_to_all(out_images, "space", split_axis=1, concat_axis=0, tiled=True),
        lax.all_to_all(grad_local, "space", split_axis=1, concat_axis=0, tiled=True),
    )
    local_grads = (grad_kernel, grad_vectors, grad_up, grad_upbias, grad_down)
    summed = lax.psum(
        (local_grads[0], local_grads[1], local_grads[2], local_grads[3], local_grads[4]),
        ("dp", "space"),
    )
    total_squares = sum((jnp.sum(g * g) for g in summed))
    owner = lax.axis_index(("dp", "space"))
    shard_grads = (
        lax.dynamic_slice_in_dim(
            summed[0], owner * depth_kernel.shape[1], depth_kernel.shape[1], 1
        ),
        lax.dynamic_slice_in_dim(
            summed[1], owner * block_vectors.shape[1], block_vectors.shape[1], 1
        ),
        lax.dynamic_slice_in_dim(summed[2], owner * up_weight.shape[1], up_weight.shape[1], 1),
        lax.dynamic_slice_in_dim(summed[3], owner * up_bias.shape[0], up_bias.shape[0], 0),
        lax.dynamic_slice_in_dim(summed[4], owner * down_weight.shape[0], down_weight.shape[0], 0),
    )
    grad_norm = jnp.sqrt(total_squares)
    factor = clip_limit / jnp.maximum(grad_norm, clip_limit)
    states = (
        (depth_kernel, kernel_moment, kernel_square),
        (block_vectors, vector_moment, vector_square),
        (up_weight, up_moment, up_square),
        (up_bias, bias_moment, bias_square),
        (down_weight, down_moment, down_square),
    )
    results = []
    for (weight, moment, square), grad_part, step_rate in zip(states, shard_grads, step_rates):
        results.extend(adam_update(weight, moment, square, grad_part, factor, step_rate))
    return (
        out_tiles,
        grad_tiles,
        results[0],
        results[1],
        results[2],
        results[3],
        results[4],
        results[5],
        results[6],
        results[7],
        results[8],
        results[9],
        results[10],
        results[11],
        results[12],
        results[13],
        results[14],
        grad_norm,
    )


def solution(mesh):
    in_specs = (
        P("dp", "space", None, None),
        P("dp", "space", None, None),
        P("dp"),
        P("dp"),
        P(None, ("dp", "space")),
        P(None, ("dp", "space")),
        P(None, ("dp", "space")),
        P(None, ("dp", "space")),
        P(None, ("dp", "space")),
        P(None, ("dp", "space")),
        P(None, ("dp", "space")),
        P(None, ("dp", "space")),
        P(None, ("dp", "space")),
        P(("dp", "space")),
        P(("dp", "space")),
        P(("dp", "space")),
        P(("dp", "space"), None),
        P(("dp", "space"), None),
        P(("dp", "space"), None),
    )
    out_specs = (
        P("dp", "space", None, None),
        P("dp", "space", None, None),
        P(None, ("dp", "space")),
        P(None, ("dp", "space")),
        P(None, ("dp", "space")),
        P(None, ("dp", "space")),
        P(None, ("dp", "space")),
        P(None, ("dp", "space")),
        P(None, ("dp", "space")),
        P(None, ("dp", "space")),
        P(None, ("dp", "space")),
        P(("dp", "space")),
        P(("dp", "space")),
        P(("dp", "space")),
        P(("dp", "space"), None),
        P(("dp", "space"), None),
        P(("dp", "space"), None),
        P(),
    )
    return jax.shard_map(body, mesh=mesh, in_specs=in_specs, out_specs=out_specs, check_vma=False)
```

profile of v0, /device:TPU:12, one launch (start us, length us, event | category | flops | bytes accessed | tf_op | source)
XLA Modules:
  0.0 850.3 jit_solution(6092713917045323219)
XLA Ops:
  7.2 4.4 all-to-all-start
  13.1 38.7 %all-to-all-done = bf16[32,6,24,384]{3,2,1,0:T(8,128)(2,1)S(1)} async-done(((bf16[32,6,24,384]{3,2,1,0:T(8,128)(2,1)}), bf16[32,6,24,384]{3,2,1,0:T(8,128)(2,1)S(1)}, u32[]{:S(2)}, u32[]{:S(2)}) %all-to-all-start) | async-done | bytes 3538976 | tf_op jit(solution)/shard_map/all_to_all | solution.py:89
  51.9 6.4 all-to-all-start.2
  59.8 64.6 %all-gather = f32[32,12,5]{1,2,0:T(8,128)S(1)} all-gather(f32[1,12,5]{1,2,0:T(8,128)S(1)} %bitcast.83), channel_id=1, replica_groups=mesh['dp'=8,'space'=4] {'dp','space'}, dimensions={0}, use_global_device_ids=true | all-gather | bytes 7920 | tf_op jit(solution)/shard_map/all_gather | solution.py:84
  126.6 43.0 %all-gather.1 = f32[32,12,49]{2,1,0:T(8,128)} all-gather(f32[1,12,49]{2,1,0:T(8,128)S(1)} %bitcast.81), channel_id=1, replica_groups=mesh['dp'=8,'space'=4] {'dp','space'}, dimensions={0}, use_global_device_ids=true | all-gather | bytes 77616 | tf_op jit(solution)/shard_map/all_gather | solution.py:83
  171.6 45.5 %all-reduce.4 = f32[1536]{0:T(1024)} all-reduce(f32[1536]{0:T(1024)S(1)} %dynamic-update-slice), channel_id=1, replica_groups=mesh['dp'=8,'space'=4] {'dp','space'}, use_global_device_ids=true, to_apply=%add.4 | all-reduce | flops 1536 | bytes 12288
  229.4 5.5 copy.165
  238.3 59.4 %fusion.231 = (f32[8,24,24]{2,1,0:T(8,128)S(1)}, f32[8,24,24,384]{3,2,1,0:T(8,128)S(1)}) fusion(f32[384]{0:T(512)} %get-tuple-element.179, f32[384]{0:T(512)S(1)} %copy-done.48, f32[384]{0:T(512)S(1)} %copy-done.49, f32[384]{0:T(512)S(1)} %copy-done.50, bf16[8,30,24,384]{3,2,1,0:T(8,128)(2,1)S(1)} %pad.17, f32[384]{0:T(512)S(1)} %copy-done.51, ...), kind=kLoop, calls=%fused_computation.507 | loop fusion | flops 267185664 | bytes 36440576 | tf_op jit(solution)/shard_map/reduce_sum | solution.py:106
  302.8 18.7 %multiply_convert_fusion = (bf16[8,24,24,1536]{3,2,1,0:T(8,128)(2,1)}, f32[8,24,24,1536]{3,2,1,0:T(8,128)}) fusion(f32[1536]{0:T(1024)S(1)} %copy-done.85, bf16[384,1536]{0,1:T(8,128)(2,1)} %all-gather.5.cloned.1.call-done, f32[8,24,24,384]{3,2,1,0:T(8,128)} %copy-done.1, f32[384]{0:T(512)} %get-tuple-element.177, f32[384]{0:T(512)S(1)} %copy-done.64, ...), kind=kOutput, calls=%fused_computation.49 | convolution fusion | flops 5487132672 | bytes 50770944 | tf_op jit(solution)/shard_map/nijc,ch->nijh/dot_general | solution.py:113
  321.5 16.5 %multiply_reduce_fusion = (f32[384]{0:T(512)}, bf16[8,24,24,384]{3,2,1,0:T(8,128)(2,1)}, bf16[8,24,24,384]{3,2,1,0:T(8,128)(2,1)S(1)}) fusion(f32[8,24,24,384]{3,2,1,0:T(8,128)} %bitcast.75, f32[384]{0:T(512)} %get-tuple-element.176, f32[8,24,24]{2,1,0:T(8,128)} %and_select_fusion.1, f32[384]{0:T(512)S(1)} %copy-done.62, ...), kind=kOutput, calls=%fused_computation.387 | convolution fusion | flops 5455281664 | bytes 33053184 | tf_op jit(solution)/shard_map/nijh,hc->nijc/dot_general | solution.py:118
  338.0 11.9 %fusion.203 = f32[1536,384]{1,0:T(8,128)} fusion(bf16[8,24,24,384]{3,2,1,0:T(8,128)(2,1)S(1)} %get-tuple-element.205, bf16[8,24,24,1536]{3,2,1,0:T(8,128)(2,1)} %get-tuple-element.208), kind=kOutput, calls=%fused_computation.401 | convolution fusion | flops 5435817984 | bytes 20054016 | tf_op jit(solution)/shard_map/nijh,nijc->hc/dot_general | solution.py:128
  349.9 21.6 %convert_reduce_fusion = (f32[1536]{0:T(1024)}, bf16[8,24,24,1536]{3,2,1,0:T(8,128)(2,1)}) fusion(f32[8,24,24,1536]{3,2,1,0:T(8,128)} %get-tuple-element.209, f32[1536]{0:T(1024)S(1)} %copy-done.85, bf16[8,24,24,384]{3,2,1,0:T(8,128)(2,1)S(1)} %get-tuple-element.205, bf16[1536,384]{1,0:T(8,128)(2,1)S(1)} %copy-done.112), kind=kOutput, calls=%fused_computation.48 | convolution fusion | flops 5527828992 | bytes 47198208 | tf_op jit(solution)/shard_map/nijc,hc->nijh/dot_general | solution.py:129
  371.5 16.5 %fusion.208 = f32[384,1536]{0,1:T(8,128)} fusion(bf16[8,24,24,1536]{3,2,1,0:T(8,128)(2,1)} %get-tuple-element.212, f32[8,24,24,384]{3,2,1,0:T(8,128)} %copy-done.1, f32[384]{0:T(512)S(1)} %copy-done.106, f32[384]{0:T(512)S(1)} %copy-done.64, f32[8,24,24]{2,1,0:T(8,128)S(1)} %copy-done.11, f32[8,24,24]{2,1,0:T(8,128)S(1)} %copy-done.8), kind=kOutput, calls=%fused_computation.402 | convolution fusion | flops 5444665344 | bytes 23632896 | tf_op jit(solution)/shard_map/nijc,nijh->ch/dot_general | solution.py:134
  388.0 15.5 %multiply_reduce_fusion.1 = (f32[384]{0:T(512)}, f32[8,24,24]{2,1,0:T(8,128)S(1)}, f32[8,24,24]{2,1,0:T(8,128)S(1)}, f32[384]{0:T(512)}, f32[8,24,24,384]{3,2,1,0:T(8,128)}) fusion(f32[8,24,24,384]{3,2,1,0:T(8,128)} %copy-done.1, f32[8,24,24]{2,1,0:T(8,128)S(1)} %copy-done.11, f32[8,24,24]{2,1,0:T(8,128)S(1)} %copy-done.8, f32[384]{0:T(512)S(1)} %copy-done.64, ...), kind=kOutput, calls=%fused_computation.389 | convolution fusion | flops 5451732992 | bytes 29569536 | tf_op jit(solution)/shard_map/nijh,ch->nijc/dot_general | solution.py:136
  404.2 36.5 %fusion.105 = (f32[384]{0:T(512)}, f32[384]{0:T(512)}, f32[384]{0:T(512)}, f32[384]{0:T(512)}, f32[384]{0:T(512)}, /*index=5*/f32[384]{0:T(512)}, f32[384]{0:T(5...) fusion(bf16[8,30,24,384]{3,2,1,0:T(8,128)(2,1)} %copy-done, ...), kind=kLoop, calls=%fused_computation.291 | loop fusion | flops 107930880 | bytes 25760256 | tf_op jit(solution)/shard_map/reduce_sum | solution.py:37
  440.7 8.9 %fusion.102 = (f32[384]{0:T(512)}, f32[384]{0:T(512)}, f32[384]{0:T(512)}, f32[384]{0:T(512)}, f32[384]{0:T(512)}, /*index=5*/f32[384]{0:T(512)}, f32[384]{0:T(512)}, f32[384]{0:T(512)}) fusion(f32[8,24,24,384]{3,2,1,0:T(8,128)} %get-tuple-element.200, bf16[8,24,24,384]{3,2,1,0:T(8,128)(2,1)S(1)} %copy-done.3), kind=kLoop, calls=%fused_computation.288 | loop fusion | flops 38925312 | bytes 10629120 | tf_op jit(solution)/shard_map/reduce_sum | solution.py:37
  449.6 8.6 %fusion.40 = (f32[384]{0:T(512)}, f32[384]{0:T(512)}, f32[384]{0:T(512)}, f32[384]{0:T(512)S(1)}, f32[384]{0:T(512)S(1)}, /*index=5*/f32[384]{0:T(512)S(1)}) fusion(f32[8,24,24,384]{3,2,1,0:T(8,128)} %get-tuple-element.200, bf16[8,30,24,384]{3,2,1,0:T(8,128)(2,1)S(1)} %bitcast.71), kind=kLoop, calls=%fused_computation.226 | loop fusion | flops 31848192 | bytes 11510784 | tf_op jit(solution)/shard_map/reduce_sum | solution.py:37
  458.2 33.2 %fusion.84 = (f32[384]{0:T(512)}, f32[384]{0:T(512)}, f32[384]{0:T(512)}, f32[384]{0:T(512)}, f32[384]{0:T(512)}, /*index=5*/f32[384]{0:T(512)}, f32[384]{0:T(51...) fusion(f32[8,24,24,384]{3,2,1,0:T(8,128)} %get-tuple-element.20, ...), kind=kLoop, calls=%fused_computation.270 | loop fusion | flops 95544576 | bytes 11529216 | tf_op jit(solution)/shard_map/reduce_sum | solution.py:37
  491.8 7.1 pad.19
  529.1 9.3 %stack.217 = f32[49,384]{1,0:T(8,128)} concatenate(f32[1,384]{1,0:T(1,128)S(1)} %stack.168, f32[1,384]{1,0:T(1,128)S(1)} %stack.169, f32[1,384]{1,0:T(1,128)} %stack.170, f32[1,384]{1,0:T(1,128)} %stack.171, f32[1,384]{1,0:T(1,128)} %stack.172, f32[1,384]{1,0:T(1,128)} %stack.173, f32[1,384]{1,0:T(1,128)} %stack.174, f32[1,384]{1,0:T(1,128)} %stack.175, f32[1,384]{1,0:T(1,128)} %stack.176, ...), dimensions={0} | concatenate | bytes 150528 | tf_op jit(solution)/shard_map/stack | solution.py:44
  547.1 184.0 %fusion.195 = bf16[8,24,24,384]{3,2,1,0:T(8,128)(2,1)} fusion(f32[8,24,24,384]{3,2,1,0:T(8,128)} %bitcast.76, f32[8,30,24,384]{3,2,1,0:T(8,128)} %pad.19, f32[8,24,24,384]{3,2,1,0:T(8,128)} %get-tuple-element.200, f32[8,24,24]{2,1,0:T(8,128)} %get-tuple-element.206, f32[384]{0:T(512)} %get-tuple-element.127, f32[384]{0:T(512)} %get-tuple-element.128, ...), kind=kLoop, calls=%fused_computation.381 | loop fusion | flops 176947200 | bytes 69206016 | tf_op jit(solution)/shard_map/convert_element_type | solution.py:150
  731.1 4.5 copy.166
  735.6 4.7 all-to-all-start.3
  747.5 67.7 %all-reduce.5 = (f32[5,384]{1,0:T(8,128)}, f32[1536]{0:T(1024)}) all-reduce(f32[5,384]{1,0:T(8,128)S(1)} %stack.223, f32[1536]{0:T(1024)} %get-tuple-element.211), channel_id=1, replica_groups=mesh['dp'=8,'space'=4] {'dp','space'}, use_global_device_ids=true, to_apply=%region_60.61 | all-reduce | flops 3456 | bytes 27648 | tf_op jit(solution)/shard_map/psum | solution.py:158
  (341 shorter events, 97.8 us)
Async XLA Ops:
  7.2 52.6 %copy-start.60 = (f32[5,12]{1,0:T(8,128)S(1)}, f32[5,12]{1,0:T(8,128)}, u32[]{:S(2)}) copy-start(f32[5,12]{1,0:T(8,128)} %param.26) | copy-start | bytes 724
  7.2 119.4 %copy-start.12 = (f32[49,12]{0,1:T(8,128)S(1)}, f32[49,12]{0,1:T(8,128)}, u32[]{:S(2)}) copy-start(f32[49,12]{0,1:T(8,128)} %param.23) | copy-start | bytes 7060
  7.2 164.1 %copy-start.110 = (f32[48]{0:T(128)S(1)}, f32[48]{0:T(128)}, u32[]{:S(2)}) copy-start(f32[48]{0:T(128)} %param.32) | copy-start | bytes 580
  7.2 44.6 %all-to-all-start = ((bf16[32,6,24,384]{3,2,1,0:T(8,128)(2,1)}), bf16[32,6,24,384]{3,2,1,0:T(8,128)(2,1)S(1)}, u32[]{:S(2)}, u32[]{:S(2)}) async-start(bf16[32,6,24,384]{3,2,1,0:T(8,128)(2,1)} %param.19), calls=%async_computation | async-start | bytes 7077888 | tf_op jit(solution)/shard_map/all_to_all | solution.py:89
  11.6 291.2 %all-gather.5.cloned.1.call-start = ((), (), s32[]{:S(2)}) async-start(), calls=%async_computation.4 | async-start | bytes 1216512 | tf_op jit(solution)/shard_map/all_gather | solution.py:79
  51.9 74.8 %copy-start.4 = (bf16[32,6,24,384]{3,2,1,0:T(8,128)(2,1)}, bf16[32,6,24,384]{3,2,1,0:T(8,128)(2,1)S(1)}, u32[]{:S(2)}) copy-start(bf16[32,6,24,384]{3,2,1,0:T(8,128)(2,1)S(1)} %all-to-all-done) | copy-start | bytes 10616836
  51.9 177.5 %all-to-all-start.2 = ((bf16[32,6,24,384]{3,2,1,0:T(8,128)(2,1)}), bf16[32,6,24,384]{3,2,1,0:T(8,128)(2,1)}, u32[]{:S(2)}, u32[]{:S(2)}) async-start(bf16[32,6,24,384]{3,2,1,0:T(8,128)(2,1)} %param.20), calls=%async_computation.2 | async-start | bytes 7077888 | tf_op jit(solution)/shard_map/all_to_all | solution.py:90
  58.2 263.3 %all-gather.7.cloned.1.call-start = ((), (), s32[]{:S(2)}) async-start(), calls=%async_computation.5 | async-start | bytes 1216512 | tf_op jit(solution)/shard_map/all_gather | solution.py:80
  236.5 61.2 %copy-start = (bf16[8,30,24,384]{3,2,1,0:T(8,128)(2,1)}, bf16[8,30,24,384]{3,2,1,0:T(8,128)(2,1)S(1)}, u32[]{:S(2)}) copy-start(bf16[8,30,24,384]{3,2,1,0:T(8,128)(2,1)S(1)} %pad.17) | copy-start | bytes 13271044
  404.2 36.5 %copy-start.3 = (bf16[8,24,24,384]{3,2,1,0:T(8,128)(2,1)S(1)}, bf16[8,24,24,384]{3,2,1,0:T(8,128)(2,1)}, u32[]{:S(2)}) copy-start(bf16[8,24,24,384]{3,2,1,0:T(8,128)(2,1)} %copy-done.2) | copy-start | bytes 10616836
  491.7 32.3 %copy-start.95 = (f32[384]{0:T(512)S(1)}, f32[384]{0:T(512)}, u32[]{:S(2)}) copy-start(f32[384]{0:T(512)} %get-tuple-element.101) | copy-start | bytes 4612
  491.7 32.9 %copy-start.94 = (f32[384]{0:T(512)S(1)}, f32[384]{0:T(512)}, u32[]{:S(2)}) copy-start(f32[384]{0:T(512)} %get-tuple-element.102) | copy-start | bytes 4612
  491.7 33.4 %copy-start.93 = (f32[384]{0:T(512)S(1)}, f32[384]{0:T(512)}, u32[]{:S(2)}) copy-start(f32[384]{0:T(512)} %get-tuple-element.103) | copy-start | bytes 4612
  491.7 34.0 %copy-start.92 = (f32[384]{0:T(512)S(1)}, f32[384]{0:T(512)}, u32[]{:S(2)}) copy-start(f32[384]{0:T(512)} %get-tuple-element.104) | copy-start | bytes 4612
  491.7 34.5 %copy-start.91 = (f32[384]{0:T(512)S(1)}, f32[384]{0:T(512)}, u32[]{:S(2)}) copy-start(f32[384]{0:T(512)} %get-tuple-element.105) | copy-start | bytes 4612
  491.7 35.1 %copy-start.90 = (f32[384]{0:T(512)S(1)}, f32[384]{0:T(512)}, u32[]{:S(2)}) copy-start(f32[384]{0:T(512)} %get-tuple-element.106) | copy-start | bytes 4612
  491.7 35.7 %copy-start.89 = (f32[384]{0:T(512)S(1)}, f32[384]{0:T(512)}, u32[]{:S(2)}) copy-start(f32[384]{0:T(512)} %get-tuple-element.107) | copy-start | bytes 4612
  491.7 36.2 %copy-start.88 = (f32[384]{0:T(512)S(1)}, f32[384]{0:T(512)}, u32[]{:S(2)}) copy-start(f32[384]{0:T(512)} %get-tuple-element.108) | copy-start | bytes 4612
  491.7 36.8 %copy-start.87 = (f32[384]{0:T(512)S(1)}, f32[384]{0:T(512)}, u32[]{:S(2)}) copy-start(f32[384]{0:T(512)} %get-tuple-element.109) | copy-start | bytes 4612
  491.8 48.4 %copy-start.6 = (bf16[8,24,24,384]{3,2,1,0:T(8,128)(2,1)S(1)}, bf16[8,24,24,384]{3,2,1,0:T(8,128)(2,1)}, u32[]{:S(2)}) copy-start(bf16[8,24,24,384]{3,2,1,0:T(8,128)(2,1)} %get-tuple-element.204) | copy-start | bytes 10616836
  542.6 193.0 %all-to-all-start.1 = ((bf16[8,24,24,384]{3,2,0,1:T(8,128)(2,1)}), bf16[8,24,24,384]{3,2,0,1:T(8,128)(2,1)S(1)}, u32[]{:S(2)}, u32[]{:S(2)}) async-start(bf16[8,24,24,384]{3,2,0,1:T(8,128)(2,1)} %copy.163), calls=%async_computation.1 | async-start | bytes 7077888 | tf_op jit(solution)/shard_map/all_to_all | solution.py:154
  546.3 271.5 %all-reduce.9.cloned.1.call-start = ((), (), s32[]{:S(2)}) async-start(), calls=%async_computation.6 | async-start | bytes 9830400 | tf_op jit(solution)/shard_map/psum | solution.py:158
  735.6 102.6 %all-to-all-start.3 = ((bf16[8,24,24,384]{3,2,0,1:T(8,128)(2,1)}), bf16[8,24,24,384]{3,2,0,1:T(8,128)(2,1)}, u32[]{:S(2)}, u32[]{:S(2)}) async-start(bf16[8,24,24,384]{3,2,0,1:T(8,128)(2,1)} %copy.166), calls=%async_computation.3 | async-start | bytes 7077888 | tf_op jit(solution)/shard_map/all_to_all | solution.py:155
  743.0 86.8 %copy-start.61 = (f32[5,12]{1,0:T(8,128)S(1)}, f32[5,12]{1,0:T(8,128)}, u32[]{:S(2)}) copy-start(f32[5,12]{1,0:T(8,128)} %param.26) | copy-start | bytes 724
  (98 other events, 984.8 us)
Sparse Core Ops, SparseCore 0:
  15.9 54.4 all-gather.4
  73.9 53.8 all-gather.6
  553.3 147.8 all-reduce.8
where the time goes:
time: 862 us; the launch traced here: 850 us
  other arithmetic  362 us (42%)
  blocking collectives  221 us (26%)
  matrix products  101 us (12%)
  local copies, waits for them, and re-layouts  88.7 us (10%)
  waiting for transfers between devices  39.5 us (5%)
  between operations  19.9 us (2%)
  starting transfers between devices  19.2 us (2%)
    convert_element_type x1, other arithmetic, body(): (grad_out + pixel_mask[..., None] * grad_u).astype(jnp.bfloat16)  184 us
    reduce_sum x4, other arithmetic, kernel_grad(): jnp.sum(wide[:, row_off:row_off + out_rows, col_off:col_off + out_cols, :...  87.2 us
    psum x1, blocking collectives, body(): lax.psum((local_grads[0], local_grads[1], local_grads[2], local_grads[3],...  67.7 us
    all_gather x1, blocking collectives, body(): lax.all_gather(block_vectors, ('dp', 'space'), axis=1, tiled=True)  64.6 us
    reduce_sum x1, other arithmetic, body(): chan_mean = jnp.mean(conv, axis=-1, keepdims=True)  59.4 us
    unnamed x1, blocking collectives  45.5 us
    all_gather x1, blocking collectives, body(): lax.all_gather(depth_kernel, ('dp', 'space'), axis=1, tiled=True)  43 us
    another operation x51, local copies, waits for them, and re-layouts, kernel_grad(): return jnp.stack(pieces)  41.1 us
  transfers between devices with their start and end apart: 7, of which 1 were waited for; matrix products, arithmetic and copies ran while one was open for 38% of the time, Pallas kernels for 0%

commit v1 on v0

--- a/solution.py
+++ b/solution.py
@@ -86,7 +86,12 @@
     )
     map_side = images.shape[2]
     local_images, local_cot = (
-        lax.all_to_all(images, "space", split_axis=0, concat_axis=1, tiled=True),
+        jnp.concatenate(
+            lax.all_to_all(
+                jnp.stack(jnp.split(images, lax.axis_size("space"), axis=0)), "space", 0, 0
+            ),
+            axis=1,
+        ),
         lax.all_to_all(cotangent, "space", split_axis=0, concat_axis=1, tiled=True),
     )
     img_count = local_images.shape[0]

time: 862 us -> 859 us (level)
  no operation moved by 1% of the time
where the time goes in v1:
time: 859 us; the launch traced here: 855 us
  other arithmetic  364 us (42%)
  blocking collectives  221 us (26%)
  matrix products  101 us (12%)
  local copies, waits for them, and re-layouts  91 us (11%)
  waiting for transfers between devices  39.5 us (5%)
  between operations  19.7 us (2%)
  starting transfers between devices  19.2 us (2%)
    convert_element_type x1, other arithmetic, body(): (grad_out + pixel_mask[..., None] * grad_u).astype(jnp.bfloat16)  184 us
    reduce_sum x4, other arithmetic, kernel_grad(): jnp.sum(wide[:, row_off:row_off + out_rows, col_off:col_off + out_cols, :...  87.2 us
    psum x1, blocking collectives, body(): lax.psum((local_grads[0], local_grads[1], local_grads[2], local_grads[3],...  67.7 us
    all_gather x1, blocking collectives, body(): lax.all_gather(block_vectors, ('dp', 'space'), axis=1, tiled=True)  64.6 us
    reduce_sum x1, other arithmetic, body(): chan_mean = jnp.mean(conv, axis=-1, keepdims=True)  59.4 us
    unnamed x1, blocking collectives  45.7 us
    all_gather x1, blocking collectives, body(): lax.all_gather(depth_kernel, ('dp', 'space'), axis=1, tiled=True)  43 us
    another operation x51, local copies, waits for them, and re-layouts, kernel_grad(): return jnp.stack(pieces)  41.1 us
  transfers between devices with their start and end apart: 7, of which 1 were waited for; matrix products, arithmetic and copies ran while one was open for 38% of the time, Pallas kernels for 0%

profile of v1, /device:TPU:12, one launch (start us, length us, event | category | flops | bytes accessed | tf_op | source)
XLA Modules:
  0.0 854.7 jit_solution(6520246456851592320)
XLA Ops:
  11.6 4.3 all-to-all-start
  17.5 38.7 %all-to-all-done = bf16[4,8,6,24,384]{4,3,2,1,0:T(8,128)(2,1)S(1)} async-done(((bf16[4,8,6,24,384]{4,3,2,1,0:T(8,128)(2,1)}), bf16[4,8,6,24,384]{4,3,2,1,0:T(8,128)(2,1)S(1)}, u32[]{:S(2)}, u32[]{:S(2)}) %all-to-all-start) | async-done | bytes 3538976 | tf_op jit(solution)/shard_map/all_to_all | solution.py:90
  56.2 6.4 all-to-all-start.2
  64.2 64.6 %all-gather = f32[32,12,5]{1,2,0:T(8,128)S(1)} all-gather(f32[1,12,5]{1,2,0:T(8,128)S(1)} %bitcast.89), channel_id=1, replica_groups=mesh['dp'=8,'space'=4] {'dp','space'}, dimensions={0}, use_global_device_ids=true | all-gather | bytes 7920 | tf_op jit(solution)/shard_map/all_gather | solution.py:84
  131.0 43.0 %all-gather.1 = f32[32,12,49]{2,1,0:T(8,128)} all-gather(f32[1,12,49]{2,1,0:T(8,128)S(1)} %bitcast.87), channel_id=1, replica_groups=mesh['dp'=8,'space'=4] {'dp','space'}, dimensions={0}, use_global_device_ids=true | all-gather | bytes 77616 | tf_op jit(solution)/shard_map/all_gather | solution.py:83
  175.9 45.7 %all-reduce.4 = f32[1536]{0:T(1024)} all-reduce(f32[1536]{0:T(1024)S(1)} %dynamic-update-slice), channel_id=1, replica_groups=mesh['dp'=8,'space'=4] {'dp','space'}, use_global_device_ids=true, to_apply=%add.4 | all-reduce | flops 1536 | bytes 12288
  233.9 5.5 copy.165
  242.8 59.4 %fusion.231 = (f32[8,24,24]{2,1,0:T(8,128)S(1)}, f32[8,24,24,384]{3,2,1,0:T(8,128)S(1)}) fusion(f32[384]{0:T(512)} %get-tuple-element.179, f32[384]{0:T(512)S(1)} %copy-done.48, f32[384]{0:T(512)S(1)} %copy-done.49, f32[384]{0:T(512)S(1)} %copy-done.50, bf16[8,30,24,384]{3,2,1,0:T(8,128)(2,1)S(1)} %pad.17, f32[384]{0:T(512)S(1)} %copy-done.51, ...), kind=kLoop, calls=%fused_computation.512 | loop fusion | flops 267185664 | bytes 36440576 | tf_op jit(solution)/shard_map/reduce_sum | solution.py:111
  307.4 18.7 %multiply_convert_fusion = (bf16[8,24,24,1536]{3,2,1,0:T(8,128)(2,1)}, f32[8,24,24,1536]{3,2,1,0:T(8,128)}) fusion(f32[1536]{0:T(1024)S(1)} %copy-done.85, bf16[384,1536]{0,1:T(8,128)(2,1)} %all-gather.5.cloned.1.call-done, f32[8,24,24,384]{3,2,1,0:T(8,128)} %copy-done.1, f32[384]{0:T(512)} %get-tuple-element.177, f32[384]{0:T(512)S(1)} %copy-done.64, ...), kind=kOutput, calls=%fused_computation.49 | convolution fusion | flops 5487132672 | bytes 50770944 | tf_op jit(solution)/shard_map/nijc,ch->nijh/dot_general | solution.py:118
  326.0 16.5 %multiply_reduce_fusion = (f32[384]{0:T(512)}, bf16[8,24,24,384]{3,2,1,0:T(8,128)(2,1)}, bf16[8,24,24,384]{3,2,1,0:T(8,128)(2,1)S(1)}) fusion(f32[8,24,24,384]{3,2,1,0:T(8,128)} %bitcast.81, f32[384]{0:T(512)} %get-tuple-element.176, f32[8,24,24]{2,1,0:T(8,128)} %and_select_fusion.1, f32[384]{0:T(512)S(1)} %copy-done.62, ...), kind=kOutput, calls=%fused_computation.387 | convolution fusion | flops 5455281664 | bytes 33053184 | tf_op jit(solution)/shard_map/nijh,hc->nijc/dot_general | solution.py:123
  342.5 11.9 %fusion.203 = f32[1536,384]{1,0:T(8,128)} fusion(bf16[8,24,24,384]{3,2,1,0:T(8,128)(2,1)S(1)} %get-tuple-element.205, bf16[8,24,24,1536]{3,2,1,0:T(8,128)(2,1)} %get-tuple-element.212), kind=kOutput, calls=%fused_computation.402 | convolution fusion | flops 5435817984 | bytes 20054016 | tf_op jit(solution)/shard_map/nijh,nijc->hc/dot_general | solution.py:133
  354.4 21.6 %convert_reduce_fusion = (f32[1536]{0:T(1024)}, bf16[8,24,24,1536]{3,2,1,0:T(8,128)(2,1)}) fusion(f32[8,24,24,1536]{3,2,1,0:T(8,128)} %get-tuple-element.213, f32[1536]{0:T(1024)S(1)} %copy-done.85, bf16[8,24,24,384]{3,2,1,0:T(8,128)(2,1)S(1)} %get-tuple-element.205, bf16[1536,384]{1,0:T(8,128)(2,1)S(1)} %copy-done.112), kind=kOutput, calls=%fused_computation.48 | convolution fusion | flops 5527828992 | bytes 47198208 | tf_op jit(solution)/shard_map/nijc,hc->nijh/dot_general | solution.py:134
  376.0 16.5 %fusion.208 = f32[384,1536]{0,1:T(8,128)} fusion(bf16[8,24,24,1536]{3,2,1,0:T(8,128)(2,1)} %get-tuple-element.216, f32[8,24,24,384]{3,2,1,0:T(8,128)} %copy-done.1, f32[384]{0:T(512)S(1)} %copy-done.106, f32[384]{0:T(512)S(1)} %copy-done.64, f32[8,24,24]{2,1,0:T(8,128)S(1)} %copy-done.11, f32[8,24,24]{2,1,0:T(8,128)S(1)} %copy-done.8), kind=kOutput, calls=%fused_computation.403 | convolution fusion | flops 5444665344 | bytes 23632896 | tf_op jit(solution)/shard_map/nijc,nijh->ch/dot_general | solution.py:139
  392.5 15.5 %multiply_reduce_fusion.1 = (f32[384]{0:T(512)}, f32[8,24,24]{2,1,0:T(8,128)S(1)}, f32[8,24,24]{2,1,0:T(8,128)S(1)}, f32[384]{0:T(512)}, f32[8,24,24,384]{3,2,1,0:T(8,128)}) fusion(f32[8,24,24,384]{3,2,1,0:T(8,128)} %copy-done.1, f32[8,24,24]{2,1,0:T(8,128)S(1)} %copy-done.11, f32[8,24,24]{2,1,0:T(8,128)S(1)} %copy-done.8, f32[384]{0:T(512)S(1)} %copy-done.64, ...), kind=kOutput, calls=%fused_computation.389 | convolution fusion | flops 5451732992 | bytes 29569536 | tf_op jit(solution)/shard_map/nijh,ch->nijc/dot_general | solution.py:141
  408.8 36.5 %fusion.105 = (f32[384]{0:T(512)}, f32[384]{0:T(512)}, f32[384]{0:T(512)}, f32[384]{0:T(512)}, f32[384]{0:T(512)}, /*index=5*/f32[384]{0:T(512)}, f32[384]{0:T(5...) fusion(bf16[8,30,24,384]{3,2,1,0:T(8,128)(2,1)} %copy-done, ...), kind=kLoop, calls=%fused_computation.291 | loop fusion | flops 107930880 | bytes 25760256 | tf_op jit(solution)/shard_map/reduce_sum | solution.py:37
  445.2 8.9 %fusion.102 = (f32[384]{0:T(512)}, f32[384]{0:T(512)}, f32[384]{0:T(512)}, f32[384]{0:T(512)}, f32[384]{0:T(512)}, /*index=5*/f32[384]{0:T(512)}, f32[384]{0:T(512)}, f32[384]{0:T(512)}) fusion(f32[8,24,24,384]{3,2,1,0:T(8,128)} %get-tuple-element.200, bf16[8,24,24,384]{3,2,1,0:T(8,128)(2,1)S(1)} %copy-done.3), kind=kLoop, calls=%fused_computation.288 | loop fusion | flops 38925312 | bytes 10629120 | tf_op jit(solution)/shard_map/reduce_sum | solution.py:37
  454.1 8.6 %fusion.40 = (f32[384]{0:T(512)}, f32[384]{0:T(512)}, f32[384]{0:T(512)}, f32[384]{0:T(512)S(1)}, f32[384]{0:T(512)S(1)}, /*index=5*/f32[384]{0:T(512)S(1)}) fusion(f32[8,24,24,384]{3,2,1,0:T(8,128)} %get-tuple-element.200, bf16[8,30,24,384]{3,2,1,0:T(8,128)(2,1)S(1)} %bitcast.77), kind=kLoop, calls=%fused_computation.226 | loop fusion | flops 31848192 | bytes 11510784 | tf_op jit(solution)/shard_map/reduce_sum | solution.py:37
  462.8 33.2 %fusion.84 = (f32[384]{0:T(512)}, f32[384]{0:T(512)}, f32[384]{0:T(512)}, f32[384]{0:T(512)}, f32[384]{0:T(512)}, /*index=5*/f32[384]{0:T(512)}, f32[384]{0:T(51...) fusion(f32[8,24,24,384]{3,2,1,0:T(8,128)} %get-tuple-element.20, ...), kind=kLoop, calls=%fused_computation.270 | loop fusion | flops 95544576 | bytes 11529216 | tf_op jit(solution)/shard_map/reduce_sum | solution.py:37
  496.3 7.1 pad.19
  533.7 9.3 %stack.237 = f32[49,384]{1,0:T(8,128)} concatenate(f32[1,384]{1,0:T(1,128)S(1)} %stack.188, f32[1,384]{1,0:T(1,128)S(1)} %stack.189, f32[1,384]{1,0:T(1,128)} %stack.190, f32[1,384]{1,0:T(1,128)} %stack.191, f32[1,384]{1,0:T(1,128)} %stack.192, f32[1,384]{1,0:T(1,128)} %stack.193, f32[1,384]{1,0:T(1,128)} %stack.194, f32[1,384]{1,0:T(1,128)} %stack.195, f32[1,384]{1,0:T(1,128)} %stack.196, ...), dimensions={0} | concatenate | bytes 150528 | tf_op jit(solution)/shard_map/stack | solution.py:44
  551.6 184.0 %fusion.195 = bf16[8,24,24,384]{3,2,1,0:T(8,128)(2,1)} fusion(f32[8,24,24,384]{3,2,1,0:T(8,128)} %bitcast.82, f32[8,30,24,384]{3,2,1,0:T(8,128)} %pad.19, f32[8,24,24,384]{3,2,1,0:T(8,128)} %get-tuple-element.200, f32[8,24,24]{2,1,0:T(8,128)} %get-tuple-element.210, f32[384]{0:T(512)} %get-tuple-element.127, f32[384]{0:T(512)} %get-tuple-element.128, ...), kind=kLoop, calls=%fused_computation.381 | loop fusion | flops 176947200 | bytes 69206016 | tf_op jit(solution)/shard_map/convert_element_type | solution.py:155
  735.7 4.5 copy.166
  740.1 4.7 all-to-all-start.3
  752.0 67.7 %all-reduce.5 = (f32[5,384]{1,0:T(8,128)}, f32[1536]{0:T(1024)}) all-reduce(f32[5,384]{1,0:T(8,128)S(1)} %stack.243, f32[1536]{0:T(1024)} %get-tuple-element.215), channel_id=1, replica_groups=mesh['dp'=8,'space'=4] {'dp','space'}, use_global_device_ids=true, to_apply=%region_60.61 | all-reduce | flops 3456 | bytes 27648 | tf_op jit(solution)/shard_map/psum | solution.py:163
  (343 shorter events, 102.2 us)
Async XLA Ops:
  11.6 52.5 %copy-start.60 = (f32[5,12]{1,0:T(8,128)S(1)}, f32[5,12]{1,0:T(8,128)}, u32[]{:S(2)}) copy-start(f32[5,12]{1,0:T(8,128)} %param.26) | copy-start | bytes 724
  11.6 119.4 %copy-start.12 = (f32[49,12]{0,1:T(8,128)S(1)}, f32[49,12]{0,1:T(8,128)}, u32[]{:S(2)}) copy-start(f32[49,12]{0,1:T(8,128)} %param.23) | copy-start | bytes 7060
  11.6 164.1 %copy-start.110 = (f32[48]{0:T(128)S(1)}, f32[48]{0:T(128)}, u32[]{:S(2)}) copy-start(f32[48]{0:T(128)} %param.32) | copy-start | bytes 580
  11.6 44.6 %all-to-all-start = ((bf16[4,8,6,24,384]{4,3,2,1,0:T(8,128)(2,1)}), bf16[4,8,6,24,384]{4,3,2,1,0:T(8,128)(2,1)S(1)}, u32[]{:S(2)}, u32[]{:S(2)}) async-start(bf16[4,8,6,24,384]{4,3,2,1,0:T(8,128)(2,1)} %pad_maximum_fusion), calls=%async_computation | async-start | bytes 7077888 | tf_op jit(solution)/shard_map/all_to_all | solution.py:90
  16.0 291.4 %all-gather.5.cloned.1.call-start = ((), (), s32[]{:S(2)}) async-start(), calls=%async_computation.4 | async-start | bytes 1216512 | tf_op jit(solution)/shard_map/all_gather | solution.py:79
  56.2 74.8 %copy-start.4 = (bf16[4,8,6,24,384]{4,3,2,1,0:T(8,128)(2,1)}, bf16[4,8,6,24,384]{4,3,2,1,0:T(8,128)(2,1)S(1)}, u32[]{:S(2)}) copy-start(bf16[4,8,6,24,384]{4,3,2,1,0:T(8,128)(2,1)S(1)} %all-to-all-done) | copy-start | bytes 10616836
  56.2 177.7 %all-to-all-start.2 = ((bf16[32,6,24,384]{3,2,1,0:T(8,128)(2,1)}), bf16[32,6,24,384]{3,2,1,0:T(8,128)(2,1)}, u32[]{:S(2)}, u32[]{:S(2)}) async-start(bf16[32,6,24,384]{3,2,1,0:T(8,128)(2,1)} %param.20), calls=%async_computation.2 | async-start | bytes 7077888 | tf_op jit(solution)/shard_map/all_to_all | solution.py:95
  62.6 263.4 %all-gather.7.cloned.1.call-start = ((), (), s32[]{:S(2)}) async-start(), calls=%async_computation.5 | async-start | bytes 1216512 | tf_op jit(solution)/shard_map/all_gather | solution.py:80
  241.0 61.2 %copy-start = (bf16[8,30,24,384]{3,2,1,0:T(8,128)(2,1)}, bf16[8,30,24,384]{3,2,1,0:T(8,128)(2,1)S(1)}, u32[]{:S(2)}) copy-start(bf16[8,30,24,384]{3,2,1,0:T(8,128)(2,1)S(1)} %pad.17) | copy-start | bytes 13271044
  408.8 36.5 %copy-start.3 = (bf16[8,24,24,384]{3,2,1,0:T(8,128)(2,1)S(1)}, bf16[8,24,24,384]{3,2,1,0:T(8,128)(2,1)}, u32[]{:S(2)}) copy-start(bf16[8,24,24,384]{3,2,1,0:T(8,128)(2,1)} %copy-done.2) | copy-start | bytes 10616836
  496.2 32.3 %copy-start.95 = (f32[384]{0:T(512)S(1)}, f32[384]{0:T(512)}, u32[]{:S(2)}) copy-start(f32[384]{0:T(512)} %get-tuple-element.101) | copy-start | bytes 4612
  496.2 32.9 %copy-start.94 = (f32[384]{0:T(512)S(1)}, f32[384]{0:T(512)}, u32[]{:S(2)}) copy-start(f32[384]{0:T(512)} %get-tuple-element.102) | copy-start | bytes 4612
  496.2 33.4 %copy-start.93 = (f32[384]{0:T(512)S(1)}, f32[384]{0:T(512)}, u32[]{:S(2)}) copy-start(f32[384]{0:T(512)} %get-tuple-element.103) | copy-start | bytes 4612
  496.2 34.0 %copy-start.92 = (f32[384]{0:T(512)S(1)}, f32[384]{0:T(512)}, u32[]{:S(2)}) copy-start(f32[384]{0:T(512)} %get-tuple-element.104) | copy-start | bytes 4612
  496.2 34.5 %copy-start.91 = (f32[384]{0:T(512)S(1)}, f32[384]{0:T(512)}, u32[]{:S(2)}) copy-start(f32[384]{0:T(512)} %get-tuple-element.105) | copy-start | bytes 4612
  496.3 35.1 %copy-start.90 = (f32[384]{0:T(512)S(1)}, f32[384]{0:T(512)}, u32[]{:S(2)}) copy-start(f32[384]{0:T(512)} %get-tuple-element.106) | copy-start | bytes 4612
  496.3 35.7 %copy-start.89 = (f32[384]{0:T(512)S(1)}, f32[384]{0:T(512)}, u32[]{:S(2)}) copy-start(f32[384]{0:T(512)} %get-tuple-element.107) | copy-start | bytes 4612
  496.3 36.2 %copy-start.88 = (f32[384]{0:T(512)S(1)}, f32[384]{0:T(512)}, u32[]{:S(2)}) copy-start(f32[384]{0:T(512)} %get-tuple-element.108) | copy-start | bytes 4612
  496.3 36.8 %copy-start.87 = (f32[384]{0:T(512)S(1)}, f32[384]{0:T(512)}, u32[]{:S(2)}) copy-start(f32[384]{0:T(512)} %get-tuple-element.109) | copy-start | bytes 4612
  496.3 48.4 %copy-start.6 = (bf16[8,24,24,384]{3,2,1,0:T(8,128)(2,1)S(1)}, bf16[8,24,24,384]{3,2,1,0:T(8,128)(2,1)}, u32[]{:S(2)}) copy-start(bf16[8,24,24,384]{3,2,1,0:T(8,128)(2,1)} %get-tuple-element.204) | copy-start | bytes 10616836
  547.1 193.0 %all-to-all-start.1 = ((bf16[8,24,24,384]{3,2,0,1:T(8,128)(2,1)}), bf16[8,24,24,384]{3,2,0,1:T(8,128)(2,1)S(1)}, u32[]{:S(2)}, u32[]{:S(2)}) async-start(bf16[8,24,24,384]{3,2,0,1:T(8,128)(2,1)} %copy.163), calls=%async_computation.1 | async-start | bytes 7077888 | tf_op jit(solution)/shard_map/all_to_all | solution.py:159
  550.9 271.5 %all-reduce.9.cloned.1.call-start = ((), (), s32[]{:S(2)}) async-start(), calls=%async_computation.6 | async-start | bytes 9830400 | tf_op jit(solution)/shard_map/psum | solution.py:163
  740.1 102.6 %all-to-all-start.3 = ((bf16[8,24,24,384]{3,2,0,1:T(8,128)(2,1)}), bf16[8,24,24,384]{3,2,0,1:T(8,128)(2,1)}, u32[]{:S(2)}, u32[]{:S(2)}) async-start(bf16[8,24,24,384]{3,2,0,1:T(8,128)(2,1)} %copy.166), calls=%async_computation.3 | async-start | bytes 7077888 | tf_op jit(solution)/shard_map/all_to_all | solution.py:160
  747.6 86.8 %copy-start.61 = (f32[5,12]{1,0:T(8,128)S(1)}, f32[5,12]{1,0:T(8,128)}, u32[]{:S(2)}) copy-start(f32[5,12]{1,0:T(8,128)} %param.26) | copy-start | bytes 724
  (98 other events, 984.8 us)
Sparse Core Ops, SparseCore 0:
  20.3 54.4 all-gather.4
  78.3 53.8 all-gather.6
  557.8 147.8 all-reduce.8
